TPU v7x, 32 devices: a whole 2x2x4 slice. The times are simulated.
32 devices in a mesh: dp: 8 (over y, x, core), mp: 4 (over z).
Axes of the slice: x: 2, y: 2, z: 4, core: 2. Of those that a mesh axis runs over, the one named last changes fastest.
Arguments:
- tokens: bfloat16 [8192, 1024], P('dp'), may hold values from -30 to 30
- query_key_value_weight: bfloat16 [1024, 3072], P(None, 'mp'), may hold values from -0.1875 to 0.1875
- adapter_down_weight: bfloat16 [1024, 512], P(None, 'mp'), may hold values from -0.1875 to 0.1875
- adapter_up_weight: bfloat16 [512, 3072], P('mp'), may hold values from -0.75 to 0.75
- attention_out_weight: bfloat16 [1024, 1024], P('mp'), may hold values from -0.1875 to 0.1875
- first_norm_gain: float32 [1024], replicated, may hold values from 0.5 to 1.5
- first_norm_bias: float32 [1024], replicated, may hold values from -3 to 3
- first_feed_weight: bfloat16 [1024, 4096], P(None, 'mp'), may hold values from -0.1875 to 0.1875
- first_feed_bias: float32 [4096], P('mp'), may hold values from -3 to 3
- second_feed_weight: bfloat16 [4096, 1024], P('mp'), may hold values from -0.09375 to 0.09375
- second_feed_bias: float32 [1024], replicated, may hold values from -3 to 3
- second_norm_gain: float32 [1024], replicated, may hold values from 0.5 to 1.5
- second_norm_bias: float32 [1024], replicated, may hold values from -3 to 3
- following_qkv_weight: bfloat16 [1024, 3072], P(None, 'mp'), may hold values from -0.1875 to 0.1875
- following_bias: float32 [3072], P('mp'), may hold values from -3 to 3
- request_page_count: int32 [4], replicated, may hold values from 1 to 32, 64 in all
- page_slot_table: int32 [64], replicated, may hold values from 0 to 63, each once
- request_adapter: int32 [4], replicated, may hold values from 0 to 31, as said below
Outputs:
- layer_out: bfloat16 [8192, 1024], P(('dp', 'mp'))
- next_qkv: bfloat16 [8192, 3072], P('dp', 'mp')
Inputs may be any that keep to these rules, and one draw needn't show every extreme that they name: `request_page_count`: the counts sum to 64; the longest request has exactly 32 pages. `page_slot_table`: names every page slot once. `request_adapter`: exactly min(16, 4) distinct adapters are named, adapters 0 and 31 among them; of the 8 adapters held by one index of mp at most 1 are named, and some index holds exactly 1 named ones.
All inputs are finite; a program needn't handle non-finite values.
Results may differ from a plain program's by a relative error of at most 0.015.
Values may be sent and summed in bfloat16 or wider, within the bound.
No kernel may reach another device: no remote copies, remote signals or barrier semaphores. Data moves between devices by JAX's collectives and lax.ppermute only.
A program may use at most 64 MiB of HBM per device.

v0:
```python
import math
import jax
import jax.numpy as jnp
from jax import lax
from jax.sharding import PartitionSpec as P

HEAD_DIM = 64
ADAPTER_RANK = 16
PAGE = 128


def request_slots(request_page_count, page_slot_table):
    slot_total = page_slot_table.shape[0]
    page_ends = jnp.cumsum(request_page_count)
    logical = jnp.arange(slot_total, dtype=jnp.int32)
    request_of = jnp.sum((logical[:, None] >= page_ends[None, :]).astype(jnp.int32), axis=1)
    matched = (page_slot_table[:, None] == logical[None, :]).astype(jnp.int32)
    return jnp.sum(matched * request_of[:, None], axis=0)


def layer_norm(values, gain_row, bias_row):
    average = jnp.mean(values, axis=-1, keepdims=True)
    centered = values - average
    variance = jnp.mean(centered * centered, axis=-1, keepdims=True)
    return centered * lax.rsqrt(variance + 1e-05) * gain_row + bias_row


def local(
    tokens,
    query_key_value_weight,
    adapter_down_weight,
    adapter_up_weight,
    attention_out_weight,
    first_norm_gain,
    first_norm_bias,
    first_feed_weight,
    first_feed_bias,
    second_feed_weight,
    second_feed_bias,
    second_norm_gain,
    second_norm_bias,
    following_qkv_weight,
    following_bias,
    request_page_count,
    page_slot_table,
    request_adapter,
):
    tok_rows = tokens.shape[0]
    mp_count = lax.axis_size("mp")
    dp_index = lax.axis_index("dp")
    mp_index = lax.axis_index("mp")
    kept_values = adapter_down_weight.shape[1] // ADAPTER_RANK
    adapter_count = kept_values * mp_count
    request_count = request_page_count.shape[0]
    slot_req = request_slots(request_page_count, page_slot_table)
    all_req = jnp.repeat(slot_req, PAGE, total_repeat_length=slot_req.shape[0] * PAGE)
    own_req = lax.dynamic_slice_in_dim(all_req, dp_index * tok_rows, tok_rows, 0)
    req_match = (own_req[:, None] == jnp.arange(request_count, dtype=jnp.int32)[None, :]).astype(
        jnp.int32
    )
    tok_adapter = jnp.sum(req_match * request_adapter[None, :], axis=1)
    grid_positions = jnp.dot(
        tokens,
        lax.all_gather(adapter_down_weight, "mp", axis=1, tiled=True),
        preferred_element_type=jnp.float32,
    )
    chosen = (tok_adapter[:, None] == jnp.arange(adapter_count, dtype=jnp.int32)[None, :]).astype(
        jnp.float32
    )
    low_rank = jnp.sum(
        grid_positions.reshape(tok_rows, adapter_count, ADAPTER_RANK) * chosen[:, :, None], axis=1
    )
    low_rank = low_rank.astype(jnp.bfloat16)
    upward_columns = lax.all_to_all(
        adapter_up_weight, "mp", split_axis=1, concat_axis=0, tiled=True
    )
    one_hot = tok_adapter[:, None] == jnp.arange(adapter_count, dtype=jnp.int32)[None, :]
    widened_rows = jnp.where(
        one_hot[:, :, None], low_rank[:, None, :], jnp.zeros((), jnp.bfloat16)
    ).reshape(tok_rows, adapter_count * ADAPTER_RANK)
    projected_rows = (
        jnp.dot(tokens, query_key_value_weight, preferred_element_type=jnp.float32)
        + jnp.dot(widened_rows, upward_columns, preferred_element_type=jnp.float32)
    ).astype(jnp.bfloat16)
    heads_dev = projected_rows.shape[1] // (3 * HEAD_DIM)
    per_head = projected_rows.reshape(tok_rows, heads_dev, 3, HEAD_DIM)
    queries = per_head[:, :, 0]
    key_value = per_head[:, :, 1:].reshape(tok_rows, heads_dev * 2 * HEAD_DIM)
    score_scale = HEAD_DIM ** (-0.5)

    def absorb_block(carry, portion, offset):
        running_max, denominator, numerator = carry
        length = portion.shape[0]
        split_rows = portion.reshape(length, heads_dev, 2, HEAD_DIM)
        key_block = split_rows[:, :, 0]
        value_block = split_rows[:, :, 1]
        key_req = lax.dynamic_slice_in_dim(all_req, offset, length, 0)
        allowed = (own_req[:, None] == key_req[None, :])[None]
        scores = (
            jnp.einsum("qhe,khe->hqk", queries, key_block, preferred_element_type=jnp.float32)
            * score_scale
        )
        block_max = jnp.max(jnp.where(allowed, scores, jnp.float32(-1e30)), axis=2)
        fresh_max = jnp.maximum(running_max, block_max)
        weights = jnp.where(allowed, jnp.exp(scores - fresh_max[:, :, None]), jnp.float32(0.0))
        shrink = jnp.exp(running_max - fresh_max)
        denominator = denominator * shrink + jnp.sum(weights, axis=2)
        numerator = numerator * shrink[:, :, None] + jnp.einsum(
            "hqk,khe->hqe",
            weights.astype(jnp.bfloat16),
            value_block,
            preferred_element_type=jnp.float32,
        )
        return (fresh_max, denominator, numerator)

    start_carry = (
        jnp.full((heads_dev, tok_rows), -1e30, jnp.float32),
        jnp.zeros((heads_dev, tok_rows), jnp.float32),
        jnp.zeros((heads_dev, tok_rows, HEAD_DIM), jnp.float32),
    )
    portion = lax.all_gather(key_value, "dp", axis=0, tiled=True)
    length = portion.shape[0]
    block_rows = math.gcd(length, 1024)

    def visit(block_index, inner):
        sub_rows = lax.dynamic_slice_in_dim(portion, block_index * block_rows, block_rows, 0)
        return absorb_block(inner, sub_rows, block_index * block_rows)

    final_max, denominator, numerator = lax.fori_loop(0, length // block_rows, visit, start_carry)
    context = (
        jnp.transpose(numerator / denominator[:, :, None], (1, 0, 2))
        .reshape(tok_rows, heads_dev * HEAD_DIM)
        .astype(jnp.bfloat16)
    )
    share_rows = tok_rows // mp_count
    row_base = mp_index * share_rows
    mixed = lax.psum(
        jnp.dot(context, attention_out_weight, preferred_element_type=jnp.float32).astype(
            jnp.bfloat16
        ),
        "mp",
    ).astype(jnp.float32)
    normed = layer_norm(
        tokens.astype(jnp.float32) + mixed, first_norm_gain, first_norm_bias
    ).astype(jnp.bfloat16)
    hidden = jax.nn.gelu(
        jnp.dot(normed, first_feed_weight, preferred_element_type=jnp.float32) + first_feed_bias,
        approximate=False,
    ).astype(jnp.bfloat16)
    feed = lax.psum(
        jnp.dot(hidden, second_feed_weight, preferred_element_type=jnp.float32).astype(
            jnp.bfloat16
        ),
        "mp",
    ).astype(jnp.float32)
    layer_full = layer_norm(
        normed.astype(jnp.float32) + feed + second_feed_bias, second_norm_gain, second_norm_bias
    ).astype(jnp.bfloat16)
    next_proj = (
        jnp.dot(layer_full, following_qkv_weight, preferred_element_type=jnp.float32)
        + following_bias
    ).astype(jnp.bfloat16)
    layer_rows = lax.dynamic_slice_in_dim(layer_full, row_base, share_rows, 0)
    return (layer_rows, next_proj)


def solution(mesh):
    placed = (
        P("dp", None),
        P(None, "mp"),
        P(None, "mp"),
        P("mp", None),
        P("mp", None),
        P(),
        P(),
        P(None, "mp"),
        P("mp"),
        P("mp", None),
        P(),
        P(),
        P(),
        P(None, "mp"),
        P("mp"),
        P(),
        P(),
        P(),
    )
    return jax.shard_map(
        local,
        mesh=mesh,
        in_specs=placed,
        out_specs=(P(("dp", "mp"), None), P("dp", "mp")),
        check_vma=False,
    )
```

profile of v0, /device:TPU:0, one launch (start us, length us, event | category | flops | bytes accessed | tf_op | source)
XLA Modules:
  0.0 462.3 jit_solution(4038813248734956425)
XLA Ops:
  10.2 6.3 %all-to-all-start = ((bf16[128,4,768]{0,2,1:T(8,128)(2,1)}), bf16[128,4,768]{0,2,1:T(8,128)(2,1)S(1)}, u32[]{:S(2)}, u32[]{:S(2)}) async-start(bf16[128,4,768]{0,2,1:T(8,128)(2,1)} %bitcast.154), calls=%async_computation | async-start | bytes 1572864 | tf_op jit(solution)/shard_map/all_to_all | solution.py:74
  19.6 4.5 compare_select_fusion.1
  24.1 5.8 %compare_reduce_fusion.56 = (pred[8192]{0:T(1024)(128)(4,1)S(1)}, pred[8192]{0:T(1024)(128)(4,1)S(1)}, pred[8192]{0:T(1024)(128)(4,1)S(1)}, pred[8192]{0:T(1024)...) fusion(s32[8192,1]{0,1:T(1,128)S(1)} %get-tuple-element.259), kind=kLoop, calls=%fused_computation.118 | loop fusion | flops 466944 | bytes 499712 | tf_op jit(solution)/shard_map/jit(_take)/gather | solution.py:56
  31.4 36.0 %select_select_fusion = s32[8192]{0:T(1024)S(1)} fusion(pred[8192]{0:T(1024)(128)(4,1)S(1)} %get-tuple-element.239, pred[8192]{0:T(1024)(128)(4,1)S(1)} %get-tuple-element.238, pred[8192]{0:T(1024)(128)(4,1)S(1)} %get-tuple-element.237, pred[8192]{0:T(1024)(128)(4,1)S(1)} %get-tuple-element.236, pred[8192]{0:T(1024)(128)(4,1)S(1)} %get-tuple-element.235, ...), kind=kLoop, calls=%fused_computation.126 | loop fusion | flops 540672 | bytes 532708 | tf_op jit(solution)/shard_map/jit(_take)/select_n | solution.py:56
  67.5 5.6 %fusion.72 = f32[1024,768]{0,1:T(8,128)} fusion(bf16[1024,1024]{1,0:T(8,128)(2,1)} %param.22, bf16[1024,768]{1,0:T(8,128)(2,1)} %param.23), kind=kOutput, calls=%fused_computation.176 | convolution fusion | flops 1610612736 | bytes 6815744 | tf_op jit(solution)/shard_map/dot_general | solution.py:82
  84.7 54.1 %all-gather.5.cloned.1.call-done = bf16[8192,512]{0,1:T(8,128)(2,1)} async-done(((bf16[1024,512]{0,1:T(8,128)(2,1)}), bf16[8192,512]{0,1:T(8,128)(2,1)}) %all-gather.5.cloned.1.call-update) | async-done | bytes 8388624 | tf_op jit(solution)/shard_map/all_gather | solution.py:121
  138.8 109.0 %while.19 = (s32[]{:T(128)}, f32[4,1024]{1,0:T(4,128)S(1)}, f32[4,1024]{1,0:T(4,128)S(1)}, f32[4,1024,64]{1,2,0:T(8,128)S(1)}, s32[1024]{0:T(1024)S(1)}, /*index...) while((s32[]{:T(128)}, f32[4,1024]{1,0:T(4,128)S(1)}, ...), condition=%wide.region_8.9_spmd.clone, body=%wide.region_5.8_spmd.clone.sunk | while | flops 1121734656 | bytes 60571836 | solution.py:129
  140.8 4.1 fusion.96
  148.5 3.8 fusion.99
  154.4 4.1 fusion.96
  162.2 3.8 fusion.99
  168.0 4.1 fusion.96
  181.6 4.1 fusion.96
  189.4 3.8 fusion.99
  195.3 4.1 fusion.96
  208.9 4.1 fusion.96
  216.7 3.8 fusion.99
  222.5 4.1 fusion.96
  230.3 3.8 fusion.99
  236.1 4.1 fusion.96
  243.9 3.8 fusion.99
  251.1 86.6 %all-reduce.3.cloned.1.call-done = bf16[1024,1024]{1,0:T(8,128)(2,1)} async-done(((bf16[1024,1024]{1,0:T(8,128)(2,1)}), bf16[1024,1024]{1,0:T(8,128)(2,1)}) %all-reduce.3.cloned.1.call-update) | async-done | bytes 2097168 | tf_op jit(solution)/shard_map/psum | solution.py:137
  344.5 15.8 %fusion.32 = bf16[1024,1024]{1,0:T(8,128)(2,1)} fusion(bf16[1024,1024]{1,0:T(8,128)(2,1)S(1)} %copy-done, f32[1024]{0:T(1024)S(1)} %copy-done.15, bf16[1024,1024]{1,0:T(8,128)(2,1)} %add_convert_fusion.1, bf16[1024,1024]{1,0:T(8,128)(2,1)} %param.29), kind=kOutput, calls=%fused_computation.56 | convolution fusion | flops 4365221888 | bytes 8392704 | tf_op jit(solution)/shard_map/dot_general | solution.py:151
  360.3 85.6 %all-reduce.5.cloned.1.call-done = bf16[1024,1024]{1,0:T(8,128)(2,1)} async-done(((bf16[1024,1024]{1,0:T(8,128)(2,1)}), bf16[1024,1024]{1,0:T(8,128)(2,1)}) %all-reduce.5.cloned.1.call-update) | async-done | bytes 2097168 | tf_op jit(solution)/shard_map/psum | solution.py:150
  (139 shorter events, 92.0 us)
Async XLA Ops:
  7.2 337.3 %copy-start = (bf16[1024,1024]{1,0:T(8,128)(2,1)S(1)}, bf16[1024,1024]{1,0:T(8,128)(2,1)}, u32[]{:S(2)}) copy-start(bf16[1024,1024]{1,0:T(8,128)(2,1)} %param.31) | copy-start | bytes 6291460
  7.2 60.2 %copy-start.13 = (s32[4]{0:T(128)S(1)}, s32[4]{0:T(128)}, u32[]{:S(2)}) copy-start(s32[4]{0:T(128)} %param.39) | copy-start | bytes 52
  7.2 68.2 %all-gather.3.cloned.1.call-start = ((), (), s32[]{:S(2)}) async-start(), calls=%async_computation.1 | async-start | bytes 1310720 | tf_op jit(solution)/shard_map/all_gather | solution.py:64
  10.2 62.9 %all-to-all-start = ((bf16[128,4,768]{0,2,1:T(8,128)(2,1)}), bf16[128,4,768]{0,2,1:T(8,128)(2,1)S(1)}, u32[]{:S(2)}, u32[]{:S(2)}) async-start(bf16[128,4,768]{0,2,1:T(8,128)(2,1)} %bitcast.154), calls=%async_computation | async-start | bytes 1572864 | tf_op jit(solution)/shard_map/all_to_all | solution.py:74
  16.5 122.3 %all-gather.5.cloned.1.call-start = ((), (), s32[]{:S(2)}) async-start(), calls=%async_computation.2 | async-start | bytes 9437184 | tf_op jit(solution)/shard_map/all_gather | solution.py:121
  73.1 0.9 copy-start.7
  75.4 3.8 copy-start.6
  80.3 1.1 copy-start.5
  82.8 254.9 %all-reduce.3.cloned.1.call-start = ((), (), s32[]{:S(2)}) async-start(), calls=%async_computation.3 | async-start | bytes 4194304 | tf_op jit(solution)/shard_map/psum | solution.py:137
  251.0 91.1 %copy-start.9 = (f32[1024]{0:T(1024)S(1)}, f32[1024]{0:T(1024)}, u32[]{:S(2)}) copy-start(f32[1024]{0:T(1024)} %param.28) | copy-start | bytes 12292
  251.0 91.1 %copy-start.10 = (f32[1024]{0:T(1024)S(1)}, f32[1024]{0:T(1024)}, u32[]{:S(2)}) copy-start(f32[1024]{0:T(1024)} %param.27) | copy-start | bytes 12292
  251.0 194.9 %all-reduce.5.cloned.1.call-start = ((), (), s32[]{:S(2)}) async-start(), calls=%async_computation.4 | async-start | bytes 4194304 | tf_op jit(solution)/shard_map/psum | solution.py:150
  337.6 3.0 copy-start.2
  337.6 3.5 copy-start.3
  342.0 2.4 copy-start.15
  344.5 101.4 %copy-start.8 = (f32[1024]{0:T(1024)S(1)}, f32[1024]{0:T(1024)}, u32[]{:S(2)}) copy-start(f32[1024]{0:T(1024)} %param.32) | copy-start | bytes 12292
  360.3 90.2 %copy-start.11 = (f32[1024]{0:T(1024)S(1)}, f32[1024]{0:T(1024)}, u32[]{:S(2)}) copy-start(f32[1024]{0:T(1024)} %param.34) | copy-start | bytes 12292
  360.3 90.2 %copy-start.12 = (f32[1024]{0:T(1024)S(1)}, f32[1024]{0:T(1024)}, u32[]{:S(2)}) copy-start(f32[1024]{0:T(1024)} %param.33) | copy-start | bytes 12292
  445.9 3.1 copy-start.1
  445.9 3.5 copy-start.4
  450.4 2.4 copy-start.14
  450.4 2.4 copy-start.16
Sparse Core Ops, SparseCore 0:
  9.6 44.6 all-gather.2
  82.9 55.8 all-gather.4
  251.1 86.4 all-reduce.2
  360.4 85.4 all-reduce.4
where the time goes:
time: 464 us; the launch traced here: 462 us
  waiting for transfers between devices  227 us (49%)
  other arithmetic  95.4 us (21%)
  matrix products  94.8 us (20%)
  local copies, waits for them, and re-layouts  24 us (5%)
  between operations  14.1 us (3%)
  starting transfers between devices  6.44 us (1%)
    psum x1, waiting for transfers between devices, local(): lax.psum(jnp.dot(context, attention_out_weight, preferred_element_type=jn...  86.6 us
    psum x1, waiting for transfers between devices, local(): lax.psum(jnp.dot(hidden, second_feed_weight, preferred_element_type=jnp.f...  85.6 us
    all_gather x1, waiting for transfers between devices, local(): portion = lax.all_gather(key_value, 'dp', axis=0, tiled=True)  54.1 us
    select_n x1, other arithmetic, local(): jnp.repeat(slot_req, PAGE, total_repeat_length=slot_req.shape[0] * PAGE)  36 us
    dot_general x8, matrix products, absorb_block(): jnp.einsum('qhe,khe->hqk', queries, key_block, preferred_element_type=jnp...  32.6 us
    dot_general x8, matrix products, absorb_block(): jnp.einsum('hqk,khe->hqe', weights.astype(jnp.bfloat16), value_block, pre...  30.5 us
    reduce_sum x8, other arithmetic, absorb_block(): denominator = denominator * shrink + jnp.sum(weights, axis=2)  29.3 us
    dot_general x1, matrix products, local(): jnp.dot(hidden, second_feed_weight, preferred_element_type=jnp.float32)  15.8 us
  transfers between devices with their start and end apart: 5, of which 3 were waited for; matrix products, arithmetic and copies ran while one was open for 13% of the time, Pallas kernels for 0%

commit v1 on v0

--- a/solution.py
+++ b/solution.py
@@ -134,11 +134,14 @@
     )
     share_rows = tok_rows // mp_count
     row_base = mp_index * share_rows
-    mixed = lax.psum(
-        jnp.dot(context, attention_out_weight, preferred_element_type=jnp.float32).astype(
-            jnp.bfloat16
+    mixed = jnp.sum(
+        lax.all_gather(
+            jnp.dot(context, attention_out_weight, preferred_element_type=jnp.float32).astype(
+                jnp.bfloat16
+            ),
+            "mp",
         ),
-        "mp",
+        0,
     ).astype(jnp.float32)
     normed = layer_norm(
         tokens.astype(jnp.float32) + mixed, first_norm_gain, first_norm_bias

time: 464 us -> 553 us (1.19); the launches traced: 462 us -> 543 us
  waiting for transfers between devices: 227 us -> 289 us
  local copies, waits for them, and re-layouts: 24 us -> 34.2 us
  other arithmetic: 95.4 us -> 103 us
    all_gather x0 -> x1, waiting for transfers between devices: none -> 150 us  [local(): lax.all_gather(jnp.dot(context, attention_out_weight, preferred_element_t...]
    psum x1 -> x0, waiting for transfers between devices: 86.6 us -> none  [local(): lax.psum(jnp.dot(context, attention_out_weight, preferred_element_type=jn...]
    slice x1, local copies, waits for them, and re-layouts: 1.31 us -> 11.5 us  [local(): key_value = per_head[:, :, 1:].reshape(tok_rows, heads_dev * 2 * HEAD_DIM)]
    reduce_sum x0 -> x1, other arithmetic: none -> 7.52 us  [local(): jnp.sum(lax.all_gather(jnp.dot(context, attention_out_weight, preferred_e...]
  transfers between devices with their start and end apart: 5 -> 5, of which waited for: 3 -> 3; matrix products, arithmetic and copies ran while one was open for 13% -> 11% of each run, Pallas kernels for 0% -> 0%
where the time goes in v1:
time: 553 us; the launch traced here: 543 us
  waiting for transfers between devices  289 us (52%)
  other arithmetic  103 us (19%)
  matrix products  94.9 us (17%)
  local copies, waits for them, and re-layouts  34.2 us (6%)
  between operations  14.4 us (3%)
  starting transfers between devices  6.44 us (1%)
    all_gather x1, waiting for transfers between devices, local(): lax.all_gather(jnp.dot(context, attention_out_weight, preferred_element_t...  150 us
    psum x1, waiting for transfers between devices, local(): lax.psum(jnp.dot(hidden, second_feed_weight, preferred_element_type=jnp.f...  84.9 us
    all_gather x1, waiting for transfers between devices, local(): portion = lax.all_gather(key_value, 'dp', axis=0, tiled=True)  54.1 us
    select_n x1, other arithmetic, local(): jnp.repeat(slot_req, PAGE, total_repeat_length=slot_req.shape[0] * PAGE)  36 us
    dot_general x8, matrix products, absorb_block(): jnp.einsum('qhe,khe->hqk', queries, key_block, preferred_element_type=jnp...  32.6 us
    dot_general x8, matrix products, absorb_block(): jnp.einsum('hqk,khe->hqe', weights.astype(jnp.bfloat16), value_block, pre...  30.5 us
    reduce_sum x8, other arithmetic, absorb_block(): denominator = denominator * shrink + jnp.sum(weights, axis=2)  29.3 us
    dot_general x1, matrix products, local(): jnp.dot(hidden, second_feed_weight, preferred_element_type=jnp.float32)  15.8 us
  transfers between devices with their start and end apart: 5, of which 3 were waited for; matrix products, arithmetic and copies ran while one was open for 11% of the time, Pallas kernels for 0%

profile of v1, /device:TPU:0, one launch (start us, length us, event | category | flops | bytes accessed | tf_op | source)
XLA Modules:
  0.0 542.9 jit_solution(2007371296714224089)
XLA Ops:
  10.2 6.3 %all-to-all-start = ((bf16[128,4,768]{0,2,1:T(8,128)(2,1)}), bf16[128,4,768]{0,2,1:T(8,128)(2,1)S(1)}, u32[]{:S(2)}, u32[]{:S(2)}) async-start(bf16[128,4,768]{0,2,1:T(8,128)(2,1)} %bitcast.156), calls=%async_computation | async-start | bytes 1572864 | tf_op jit(solution)/shard_map/all_to_all | solution.py:74
  19.6 4.5 compare_select_fusion.1
  24.1 5.8 %compare_reduce_fusion.56 = (pred[8192]{0:T(1024)(128)(4,1)S(1)}, pred[8192]{0:T(1024)(128)(4,1)S(1)}, pred[8192]{0:T(1024)(128)(4,1)S(1)}, pred[8192]{0:T(1024)...) fusion(s32[8192,1]{0,1:T(1,128)S(1)} %get-tuple-element.259), kind=kLoop, calls=%fused_computation.118 | loop fusion | flops 466944 | bytes 499712 | tf_op jit(solution)/shard_map/jit(_take)/gather | solution.py:56
  31.4 36.0 %select_select_fusion = s32[8192]{0:T(1024)S(1)} fusion(pred[8192]{0:T(1024)(128)(4,1)S(1)} %get-tuple-element.239, pred[8192]{0:T(1024)(128)(4,1)S(1)} %get-tuple-element.238, pred[8192]{0:T(1024)(128)(4,1)S(1)} %get-tuple-element.237, pred[8192]{0:T(1024)(128)(4,1)S(1)} %get-tuple-element.236, pred[8192]{0:T(1024)(128)(4,1)S(1)} %get-tuple-element.235, ...), kind=kLoop, calls=%fused_computation.126 | loop fusion | flops 540672 | bytes 532708 | tf_op jit(solution)/shard_map/jit(_take)/select_n | solution.py:56
  67.5 5.5 %fusion.72 = f32[1024,768]{0,1:T(8,128)} fusion(bf16[1024,1024]{1,0:T(8,128)(2,1)} %param.22, bf16[1024,768]{1,0:T(8,128)(2,1)} %param.23), kind=kOutput, calls=%fused_computation.176 | convolution fusion | flops 1610612736 | bytes 6815744 | tf_op jit(solution)/shard_map/dot_general | solution.py:82
  81.4 11.5 %slice.107 = bf16[1024,4,2,64]{0,3,2,1:T(8,128)(2,1)} slice(bf16[1024,4,3,64]{0,3,2,1:T(8,128)(2,1)S(1)} %bitcast.150), slice={[0:1024], [0:4], [1:3], [0:64]} | slice | bytes 2097152 | tf_op jit(solution)/shard_map/slice | solution.py:88
  94.9 54.1 %all-gather.7.cloned.1.call-done = bf16[8192,512]{0,1:T(8,128)(2,1)} async-done(((bf16[1024,512]{0,1:T(8,128)(2,1)}), bf16[8192,512]{0,1:T(8,128)(2,1)}) %all-gather.7.cloned.1.call-update) | async-done | bytes 8388624 | tf_op jit(solution)/shard_map/all_gather | solution.py:121
  149.0 109.0 %while.19 = (s32[]{:T(128)}, f32[4,1024]{1,0:T(4,128)S(1)}, f32[4,1024]{1,0:T(4,128)S(1)}, f32[4,1024,64]{1,2,0:T(8,128)S(1)}, s32[1024]{0:T(1024)S(1)}, /*index...) while((s32[]{:T(128)}, f32[4,1024]{1,0:T(4,128)S(1)}, ...), condition=%wide.region_8.9_spmd.clone, body=%wide.region_5.8_spmd.clone.sunk | while | flops 1121734656 | bytes 60571836 | solution.py:129
  151.0 4.1 fusion.96
  164.6 4.1 fusion.96
  178.2 4.1 fusion.96
  186.0 3.8 fusion.99
  191.9 4.1 fusion.96
  205.5 4.1 fusion.96
  219.1 4.1 fusion.96
  226.9 3.8 fusion.99
  232.7 4.1 fusion.96
  240.5 3.8 fusion.99
  246.4 4.1 fusion.96
  254.1 3.8 fusion.99
  261.4 149.7 %all-gather.9.cloned.1.call-done = bf16[4096,1024]{1,0:T(8,128)(2,1)} async-done(((bf16[1024,1024]{1,0:T(8,128)(2,1)}), bf16[4096,1024]{1,0:T(8,128)(2,1)}) %all-gather.9.cloned.1.call-update) | async-done | bytes 8388624 | tf_op jit(solution)/shard_map/all_gather | solution.py:138
  411.1 7.5 %reduce_sum.101 = bf16[1024,1024]{1,0:T(8,128)(2,1)} reduce(bf16[4,1024,1024]{2,1,0:T(8,128)(2,1)} %bitcast.149, bf16[]{:T(256)} %constant.193.clone.1), dimensions={0}, to_apply=%region_9.10 | reduce | flops 3145728 | bytes 10485762 | tf_op jit(solution)/shard_map/reduce_sum | solution.py:137
  425.5 15.8 %fusion.32 = bf16[1024,1024]{1,0:T(8,128)(2,1)} fusion(bf16[1024,1024]{1,0:T(8,128)(2,1)S(1)} %copy-done, f32[1024]{0:T(1024)S(1)} %copy-done.15, bf16[1024,1024]{1,0:T(8,128)(2,1)} %add_convert_fusion.1, bf16[1024,1024]{1,0:T(8,128)(2,1)} %param.29), kind=kOutput, calls=%fused_computation.56 | convolution fusion | flops 4365221888 | bytes 8392704 | tf_op jit(solution)/shard_map/dot_general | solution.py:154
  441.3 84.9 %all-reduce.2.cloned.1.call-done = bf16[1024,1024]{1,0:T(8,128)(2,1)} async-done(((bf16[1024,1024]{1,0:T(8,128)(2,1)}), bf16[1024,1024]{1,0:T(8,128)(2,1)}) %all-reduce.2.cloned.1.call-update) | async-done | bytes 2097168 | tf_op jit(solution)/shard_map/psum | solution.py:153
  (140 shorter events, 98.4 us)
Async XLA Ops:
  7.2 418.3 %copy-start = (bf16[1024,1024]{1,0:T(8,128)(2,1)S(1)}, bf16[1024,1024]{1,0:T(8,128)(2,1)}, u32[]{:S(2)}) copy-start(bf16[1024,1024]{1,0:T(8,128)(2,1)} %param.31) | copy-start | bytes 6291460
  7.2 60.2 %copy-start.13 = (s32[4]{0:T(128)S(1)}, s32[4]{0:T(128)}, u32[]{:S(2)}) copy-start(s32[4]{0:T(128)} %param.39) | copy-start | bytes 52
  7.2 68.2 %all-gather.5.cloned.1.call-start = ((), (), s32[]{:S(2)}) async-start(), calls=%async_computation.1 | async-start | bytes 1310720 | tf_op jit(solution)/shard_map/all_gather | solution.py:64
  10.2 62.9 %all-to-all-start = ((bf16[128,4,768]{0,2,1:T(8,128)(2,1)}), bf16[128,4,768]{0,2,1:T(8,128)(2,1)S(1)}, u32[]{:S(2)}, u32[]{:S(2)}) async-start(bf16[128,4,768]{0,2,1:T(8,128)(2,1)} %bitcast.156), calls=%async_computation | async-start | bytes 1572864 | tf_op jit(solution)/shard_map/all_to_all | solution.py:74
  16.5 132.5 %all-gather.7.cloned.1.call-start = ((), (), s32[]{:S(2)}) async-start(), calls=%async_computation.2 | async-start | bytes 9437184 | tf_op jit(solution)/shard_map/all_gather | solution.py:121
  73.1 0.9 copy-start.7
  75.4 3.8 copy-start.6
  80.3 1.1 copy-start.5
  93.0 318.1 %all-gather.9.cloned.1.call-start = ((), (), s32[]{:S(2)}) async-start(), calls=%async_computation.4 | async-start | bytes 10485760 | tf_op jit(solution)/shard_map/all_gather | solution.py:138
  261.3 264.8 %all-reduce.2.cloned.1.call-start = ((), (), s32[]{:S(2)}) async-start(), calls=%async_computation.3 | async-start | bytes 4194304 | tf_op jit(solution)/shard_map/psum | solution.py:153
  418.6 3.0 copy-start.2
  418.6 3.5 copy-start.3
  418.6 4.4 copy-start.9
  418.6 4.4 copy-start.10
  423.0 2.4 copy-start.15
  425.5 100.7 %copy-start.8 = (f32[1024]{0:T(1024)S(1)}, f32[1024]{0:T(1024)}, u32[]{:S(2)}) copy-start(f32[1024]{0:T(1024)} %param.32) | copy-start | bytes 12292
  441.2 89.5 %copy-start.11 = (f32[1024]{0:T(1024)S(1)}, f32[1024]{0:T(1024)}, u32[]{:S(2)}) copy-start(f32[1024]{0:T(1024)} %param.34) | copy-start | bytes 12292
  441.3 89.4 %copy-start.12 = (f32[1024]{0:T(1024)S(1)}, f32[1024]{0:T(1024)}, u32[]{:S(2)}) copy-start(f32[1024]{0:T(1024)} %param.33) | copy-start | bytes 12292
  526.1 3.1 copy-start.1
  526.1 3.5 copy-start.4
  530.7 2.4 copy-start.14
  530.7 2.4 copy-start.16
Sparse Core Ops, SparseCore 0:
  9.6 44.6 all-gather.4
  93.1 55.8 all-gather.6
  261.4 149.6 all-gather.8
  441.4 84.7 all-reduce.1
